TPU v7x, 32 devices: a whole 2x2x4 slice. The times are simulated.
32 devices in a mesh: mode: 8 (over y, x, core), orb: 4 (over z).
Axes of the slice: x: 2, y: 2, z: 4, core: 2. Of those that a mesh axis runs over, the one named last changes fastest.
Arguments:
- correlators: float32 [512, 2, 256, 256], P('mode', None, 'orb'), may hold values from -6 to 6
- density: float32 [2, 256, 256], P(None, 'orb'), may hold values from -6 to 6
- bare_hamiltonian: float32 [2, 256, 256], P(None, 'orb'), may hold values from -0.375 to 0.375
- coupling: float32 [512], P('mode'), may hold values from -0.25 to 0.25
- propagator: float32 [512, 512], P('mode'), may hold values from -0.25 to 0.25
Outputs:
- correlators_out: float32 [512, 2, 256, 256], P('mode', None, 'orb')
- density_out: float32 [2, 256, 256], P(None, 'orb')
All inputs are finite; a program needn't handle non-finite values.
Results may differ from a plain program's by a relative error of at most 0.0001.
Values sent between devices are 32-bit elements; how exact they have to be, the bound alone decides.
No kernel may reach another device: no remote copies, remote signals or barrier semaphores. Data moves between devices by JAX's collectives and lax.ppermute only.
A program may use at most 128 MiB of HBM per device.

v0:
```python
import jax
import jax.numpy as jnp
from jax import lax
from jax.sharding import PartitionSpec as P

time_step = 0.1
field_weight = 0.0625


def contract(form, first, second):
    return jnp.einsum(form, first, second, precision=lax.Precision.HIGHEST)


def left_product(matrix, stack):
    real = contract("ij,mjk->mik", matrix[0], stack[:, 0]) - contract(
        "ij,mjk->mik", matrix[1], stack[:, 1]
    )
    imag = contract("ij,mjk->mik", matrix[0], stack[:, 1]) + contract(
        "ij,mjk->mik", matrix[1], stack[:, 0]
    )
    return jnp.stack([real, imag], axis=1)


def right_product(stack, matrix):
    real = contract("mij,jk->mik", stack[:, 0], matrix[0]) - contract(
        "mij,jk->mik", stack[:, 1], matrix[1]
    )
    imag = contract("mij,jk->mik", stack[:, 0], matrix[1]) + contract(
        "mij,jk->mik", stack[:, 1], matrix[0]
    )
    return jnp.stack([real, imag], axis=1)


def advance(stack, commut, weights, dens):
    turned = jnp.stack([commut[:, 1], -commut[:, 0]], axis=1)
    return stack + time_step * turned + time_step * weights[:, None, None, None] * dens[None]


def modes_substep(stacks, dens, hamil, bare_full, weights):
    commut = left_product(hamil, stacks) - right_product(stacks, hamil)
    updated = advance(stacks, commut, weights, dens)
    partial_value = contract("m,mcij->cij", weights, updated)
    collision = lax.psum(partial_value, ("mode", "orb"))
    dens = dens + time_step * collision
    return (updated, dens, bare_full + field_weight * dens)


def to_whole(stacks):
    return lax.all_to_all(stacks, "orb", split_axis=0, concat_axis=2, tiled=True)


def to_split(stacks):
    return lax.all_to_all(stacks, "orb", split_axis=2, concat_axis=0, tiled=True)


def propagate(stacks, propagator):
    local_modes = stacks.shape[0]
    groups = lax.axis_size("mode")
    flat = stacks.reshape(local_modes, groups, -1)
    spread = lax.all_to_all(flat, "mode", split_axis=1, concat_axis=0, tiled=True)
    entries = spread[:, 0, :]
    mixed = contract("mn,nx->mx", lax.all_gather(propagator, "mode", axis=0, tiled=True), entries)
    returned = lax.all_to_all(mixed[:, None, :], "mode", split_axis=0, concat_axis=1, tiled=True)
    return returned.reshape(stacks.shape)


def on_device(correlators, density, bare_hamiltonian, coupling, propagator):
    dens, bare_full = (
        lax.all_gather(density, "orb", axis=1, tiled=True),
        lax.all_gather(bare_hamiltonian, "orb", axis=1, tiled=True),
    )
    hamil = bare_full + field_weight * dens
    owned = correlators.shape[0] // lax.axis_size("orb")
    weights = lax.dynamic_slice_in_dim(coupling, lax.axis_index("orb") * owned, owned, 0)
    whole = to_whole(correlators)
    for turn in range(2):
        whole, dens, hamil = modes_substep(whole, dens, hamil, bare_full, weights)
    stacks = propagate(to_split(whole), propagator)
    whole = to_whole(stacks)
    whole, dens, hamil = modes_substep(whole, dens, hamil, bare_full, weights)
    stacks = to_split(whole)
    row_count = density.shape[1]
    dens_rows = lax.dynamic_slice_in_dim(dens, lax.axis_index("orb") * row_count, row_count, 1)
    return (stacks, dens_rows)


def solution(mesh):
    in_specs = (
        P("mode", None, "orb", None),
        P(None, "orb", None),
        P(None, "orb", None),
        P("mode"),
        P("mode", None),
    )
    out_specs = (P("mode", None, "orb", None), P(None, "orb", None))
    return jax.shard_map(
        on_device, mesh=mesh, in_specs=in_specs, out_specs=out_specs, check_vma=False
    )
```

profile of v0, /device:TPU:0, one launch (start us, length us, event | category | flops | bytes accessed | tf_op | source)
XLA Modules:
  0.0 1640.5 jit_solution(9633585185455088017)
XLA Ops:
  8.0 6.5 all-to-all-start
  14.6 194.0 %all_gather.10 = f32[2,256,256]{2,1,0:T(8,128)S(1)} all-gather(f32[2,64,256]{2,1,0:T(8,128)S(1)} %copy-done.12), channel_id=1, replica_groups=mesh['mode'=8,'orb'=4] {'orb'}, dimensions={1}, use_global_device_ids=true | all-gather | bytes 655360 | tf_op jit(solution)/shard_map/all_gather | solution.py:69
  208.6 15.9 all_gather.9
  250.7 13.2 subtract_bitcast_fusion.5
  282.9 7.8 fusion.10
  291.5 130.2 %all-reduce.4.cloned.1.call-done = f32[2,256,256]{2,1,0:T(8,128)} async-done(((f32[2,256,256]{2,1,0:T(8,128)}), f32[2,256,256]{2,1,0:T(8,128)}) %all-reduce.4.cloned.1.call-update) | async-done | bytes 524304 | tf_op jit(solution)/shard_map/psum | solution.py:43
  423.8 6.1 fusion.21
  450.7 5.5 subtract_bitcast_fusion.3
  456.3 5.4 add_bitcast_fusion.3
  470.3 6.9 fusion.3
  477.2 8.3 copy.81
  485.4 186.8 %all_to_all.99 = f32[16,2,256,256]{3,0,1,2:T(8,128)S(1)} all-to-all(f32[16,2,256,256]{3,0,1,2:T(8,128)} %copy.81), channel_id=1, replica_groups=mesh['mode'=8,'orb'=4] {'orb'}, dimensions={2} | all-to-all | bytes 16777216 | tf_op jit(solution)/shard_map/all_to_all | solution.py:53
  672.3 8.3 copy.145
  680.5 9.4 reshape.18
  689.9 11.6 copy.83
  707.1 56.9 %all-gather.2.cloned.1.call-done = f32[512,512]{1,0:T(8,128)} async-done(((f32[64,512]{1,0:T(8,128)}), f32[512,512]{1,0:T(8,128)}) %all-gather.2.cloned.1.call-update) | async-done | bytes 1048592 | tf_op jit(solution)/shard_map/all_gather | solution.py:62
  764.0 40.7 %all-to-all-done.2 = f32[64,8,4096]{2,0,1:T(8,128)} async-done(((f32[64,8,4096]{2,0,1:T(8,128)}), f32[64,8,4096]{2,0,1:T(8,128)}, u32[]{:S(2)}, u32[]{:S(2)}) %all-to-all-start.2) | async-done | bytes 8388640 | tf_op jit(solution)/shard_map/all_to_all | solution.py:60
  804.7 30.3 %convolution_bitcast_fusion = f32[512,1,4096]{0,2,1:T(8,128)} fusion(f32[512,4096]{1,0:T(8,128)} %bitcast.41, f32[512,512]{1,0:T(8,128)} %all-gather.2.cloned.1.call-done), kind=kOutput, calls=%fused_computation.19 | convolution fusion | flops 12884901888 | bytes 17825792 | tf_op jit(solution)/shard_map/mn,nx->mx/dot_general | solution.py:11
  835.0 19.3 %copy.84 = f32[512,1,4096]{2,1,0:T(1,128)} copy(f32[512,1,4096]{0,2,1:T(8,128)} %convolution_bitcast_fusion) | data formatting | bytes 16777216 | tf_op jit(solution)/shard_map/broadcast_in_dim | solution.py:63
  854.3 97.8 %all_to_all.100 = f32[512,1,4096]{2,1,0:T(1,128)S(1)} all-to-all(f32[512,1,4096]{2,1,0:T(1,128)} %copy.84), channel_id=1, replica_groups=mesh['mode'=8,'orb'=4] {'mode'}, dimensions={0} | all-to-all | bytes 16777216 | tf_op jit(solution)/shard_map/all_to_all | solution.py:63
  952.1 8.1 copy.134
  960.2 8.5 copy.85
  968.6 9.4 reshape.19
  978.0 5.7 all-to-all-start.4
  983.8 12.9 fusion.8
  997.5 272.8 %all-reduce.6.cloned.1.call-done = f32[2,256,256]{2,1,0:T(8,128)} async-done(((f32[2,256,256]{2,1,0:T(8,128)}), f32[2,256,256]{2,1,0:T(8,128)}) %all-reduce.6.cloned.1.call-update) | async-done | bytes 524304 | tf_op jit(solution)/shard_map/psum | solution.py:43
  1302.0 5.5 add_bitcast_fusion.1
  1319.6 8.3 copy.95
  1327.9 5.6 all-to-all-start.5
  1333.6 12.7 fusion.6
  1347.1 272.6 %all-reduce.8.cloned.1.call-done = f32[2,256,256]{2,1,0:T(8,128)} async-done(((f32[2,256,256]{2,1,0:T(8,128)}), f32[2,256,256]{2,1,0:T(8,128)}) %all-reduce.8.cloned.1.call-update) | async-done | bytes 524304 | tf_op jit(solution)/shard_map/psum | solution.py:43
  1621.3 11.6 copy.96
  (84 shorter events, 130.1 us)
Async XLA Ops:
  8.0 6.5 copy-start.14
  8.0 6.6 copy-start.12
  8.0 200.5 %copy-start.13 = (f32[2,64,256]{2,1,0:T(8,128)S(1)}, f32[2,64,256]{2,1,0:T(8,128)}, u32[]{:S(2)}) copy-start(f32[2,64,256]{2,1,0:T(8,128)} %param.7) | copy-start | bytes 393220
  8.0 216.6 %all-to-all-start = ((f32[64,2,64,256]{3,2,1,0:T(8,128)}), f32[64,2,64,256]{3,2,1,0:T(8,128)}, u32[]{:S(2)}, u32[]{:S(2)}) async-start(f32[64,2,64,256]{3,2,1,0:T(8,128)} %param.5), calls=%async_computation | async-start | bytes 16777216 | tf_op jit(solution)/shard_map/all_to_all | solution.py:49
  14.5 407.2 %all-reduce.4.cloned.1.call-start = ((), (), s32[]{:S(2)}) async-start(), calls=%async_computation.6 | async-start | bytes 1048576 | tf_op jit(solution)/shard_map/psum | solution.py:43
  208.6 213.2 %copy-start.8 = (f32[2,256,256]{2,1,0:T(8,128)}, f32[2,256,256]{2,1,0:T(8,128)S(1)}, u32[]{:S(2)}) copy-start(f32[2,256,256]{2,1,0:T(8,128)S(1)} %all_gather.10) | copy-start | bytes 1572868
  224.5 197.2 %copy-start.9 = (f32[2,256,256]{2,1,0:T(8,128)}, f32[2,256,256]{2,1,0:T(8,128)S(1)}, u32[]{:S(2)}) copy-start(f32[2,256,256]{2,1,0:T(8,128)S(1)} %all_gather.9) | copy-start | bytes 1572868
  228.7 45.9 %copy-start = (f32[4,16,2,64,256]{4,3,0,1,2:T(8,128)}, f32[4,16,2,64,256]{4,3,0,1,2:T(8,128)S(1)}, u32[]{:S(2)}) copy-start(f32[4,16,2,64,256]{4,3,0,1,2:T(8,128)S(1)} %copy.64) | copy-start | bytes 25165828
  274.6 4.9 copy-start.5
  279.5 3.4 copy-start.1
  421.7 8.2 copy-start.2
  456.3 5.4 copy-start.7
  456.3 14.0 slice-start
  461.7 8.6 slice-start.1
  466.0 4.3 copy-start.6
  477.2 8.3 copy-start.3
  701.5 103.2 %all-to-all-start.2 = ((f32[64,8,4096]{2,0,1:T(8,128)}), f32[64,8,4096]{2,0,1:T(8,128)}, u32[]{:S(2)}, u32[]{:S(2)}) async-start(f32[64,8,4096]{2,0,1:T(8,128)} %copy.83), calls=%async_computation.2 | async-start | bytes 16777216 | tf_op jit(solution)/shard_map/all_to_all | solution.py:60
  706.5 57.5 %all-gather.2.cloned.1.call-start = ((), (), s32[]{:S(2)}) async-start(), calls=%async_computation.7 | async-start | bytes 1179648 | tf_op jit(solution)/shard_map/all_gather | solution.py:62
  978.0 293.5 %all-to-all-start.4 = ((f32[64,2,64,256]{3,2,1,0:T(8,128)}), f32[64,2,64,256]{3,2,1,0:T(8,128)}, u32[]{:S(2)}, u32[]{:S(2)}) async-start(f32[64,2,64,256]{3,2,1,0:T(8,128)} %reshape.19), calls=%async_computation.4 | async-start | bytes 16777216 | tf_op jit(solution)/shard_map/all_to_all | solution.py:49
  983.7 286.7 %copy-start.10 = (f32[2,256,256]{2,1,0:T(8,128)S(1)}, f32[2,256,256]{2,1,0:T(8,128)}, u32[]{:S(2)}) copy-start(f32[2,256,256]{2,1,0:T(8,128)} %copy-done.9) | copy-start | bytes 1572868
  983.7 286.7 %copy-start.11 = (f32[2,256,256]{2,1,0:T(8,128)S(1)}, f32[2,256,256]{2,1,0:T(8,128)}, u32[]{:S(2)}) copy-start(f32[2,256,256]{2,1,0:T(8,128)} %get-tuple-element.5) | copy-start | bytes 1572868
  983.7 286.7 %all-reduce.6.cloned.1.call-start = ((), (), s32[]{:S(2)}) async-start(), calls=%async_computation.8 | async-start | bytes 1048576 | tf_op jit(solution)/shard_map/psum | solution.py:43
  1316.4 3.3 copy-start.4
  1327.9 293.5 %all-to-all-start.5 = ((f32[16,2,256,256]{3,0,1,2:T(8,128)}), f32[16,2,256,256]{3,0,1,2:T(8,128)}, u32[]{:S(2)}, u32[]{:S(2)}) async-start(f32[16,2,256,256]{3,0,1,2:T(8,128)} %copy.95), calls=%async_computation.5 | async-start | bytes 16777216 | tf_op jit(solution)/shard_map/all_to_all | solution.py:53
  1333.5 286.2 %all-reduce.8.cloned.1.call-start = ((), (), s32[]{:S(2)}) async-start(), calls=%async_computation.9 | async-start | bytes 1048576 | tf_op jit(solution)/shard_map/psum | solution.py:43
Sparse Core Ops, SparseCore 0:
  291.7 130.0 all-reduce.3
  997.6 272.6 all-reduce.5
  1347.2 272.4 all-reduce.7
Sparse Core Ops, SparseCore 1:
  708.9 55.1 all-gather.1
where the time goes:
time: 1650 us; the launch traced here: 1640 us
  waiting for transfers between devices  774 us (47%)
  blocking collectives  494 us (30%)
  matrix products  174 us (11%)
  local copies, waits for them, and re-layouts  120 us (7%)
  other arithmetic  39.6 us (2%)
  starting transfers between devices  22.9 us (1%)
    psum x3, waiting for transfers between devices, modes_substep(): collision = lax.psum(partial_value, ('mode', 'orb'))  676 us
    all_gather x1, blocking collectives, on_device(): lax.all_gather(density, 'orb', axis=1, tiled=True)  194 us
    all_to_all x1, blocking collectives, to_split(): lax.all_to_all(stacks, 'orb', split_axis=2, concat_axis=0, tiled=True)  187 us
    dot_general x28, matrix products, contract(): return jnp.einsum(form, first, second, precision=lax.Precision.HIGHEST)  174 us
    all_to_all x1, blocking collectives, propagate(): lax.all_to_all(mixed[:, None, :], 'mode', split_axis=0, concat_axis=1, ti...  97.8 us
    all_gather x1, waiting for transfers between devices, propagate(): lax.all_gather(propagator, 'mode', axis=0, tiled=True)  56.9 us
    all_to_all x1, waiting for transfers between devices, propagate(): lax.all_to_all(flat, 'mode', split_axis=1, concat_axis=0, tiled=True)  40.7 us
  transfers between devices with their start and end apart: 8, of which 5 were waited for; matrix products, arithmetic and copies ran while one was open for 2% of the time, Pallas kernels for 0%

commit v1 on v0

--- a/solution.py
+++ b/solution.py
@@ -40,7 +40,9 @@
     commut = left_product(hamil, stacks) - right_product(stacks, hamil)
     updated = advance(stacks, commut, weights, dens)
     partial_value = contract("m,mcij->cij", weights, updated)
-    collision = lax.psum(partial_value, ("mode", "orb"))
+    collision = partial_value
+    for axis in ("orb", "mode"):
+        collision = lax.psum(collision, axis)
     dens = dens + time_step * collision
     return (updated, dens, bare_full + field_weight * dens)
 

time: 1650 us -> 1470 us (0.89)
  waiting for transfers between devices: 774 us -> 597 us
    psum x3 -> x6, waiting for transfers between devices: 676 us -> 499 us  [modes_substep(): collision = lax.psum(collision, axis)]
  transfers between devices with their start and end apart: 8 -> 11, of which waited for: 5 -> 8; matrix products, arithmetic and copies ran while one was open for 2% -> 2% of each run, Pallas kernels for 0% -> 0%
where the time goes in v1:
time: 1470 us; the launch traced here: 1460 us
  waiting for transfers between devices  597 us (41%)
  blocking collectives  495 us (34%)
  matrix products  173 us (12%)
  local copies, waits for them, and re-layouts  120 us (8%)
  other arithmetic  39.6 us (3%)
  starting transfers between devices  23.5 us (2%)
  between operations  15 us (1%)
    psum x6, waiting for transfers between devices, modes_substep(): collision = lax.psum(collision, axis)  499 us
    all_gather x1, blocking collectives, on_device(): lax.all_gather(density, 'orb', axis=1, tiled=True)  194 us
    all_to_all x1, blocking collectives, to_split(): lax.all_to_all(stacks, 'orb', split_axis=2, concat_axis=0, tiled=True)  187 us
    dot_general x28, matrix products, contract(): return jnp.einsum(form, first, second, precision=lax.Precision.HIGHEST)  173 us
    all_to_all x1, blocking collectives, propagate(): lax.all_to_all(mixed[:, None, :], 'mode', split_axis=0, concat_axis=1, ti...  97.8 us
    all_gather x1, waiting for transfers between devices, propagate(): lax.all_gather(propagator, 'mode', axis=0, tiled=True)  56.8 us
    all_to_all x1, waiting for transfers between devices, propagate(): lax.all_to_all(flat, 'mode', split_axis=1, concat_axis=0, tiled=True)  40.7 us
  transfers between devices with their start and end apart: 11, of which 8 were waited for; matrix products, arithmetic and copies ran while one was open for 2% of the time, Pallas kernels for 0%

profile of v1, /device:TPU:0, one launch (start us, length us, event | category | flops | bytes accessed | tf_op | source)
XLA Modules:
  0.0 1463.0 jit_solution(11224714549505785684)
XLA Ops:
  7.2 6.5 all-to-all-start
  13.8 194.0 %all_gather.10 = f32[2,256,256]{2,1,0:T(8,128)S(1)} all-gather(f32[2,64,256]{2,1,0:T(8,128)S(1)} %copy-done.12), channel_id=1, replica_groups=mesh['mode'=8,'orb'=4] {'orb'}, dimensions={1}, use_global_device_ids=true | all-gather | bytes 655360 | tf_op jit(solution)/shard_map/all_gather | solution.py:71
  207.7 15.9 %all_gather.9 = f32[2,256,256]{2,1,0:T(8,128)S(1)} all-gather(f32[2,64,256]{2,1,0:T(8,128)S(1)} %copy-done.13), channel_id=1, replica_groups=mesh['mode'=8,'orb'=4] {'orb'}, dimensions={1}, use_global_device_ids=true | all-gather | bytes 655360 | tf_op jit(solution)/shard_map/all_gather | solution.py:72
  249.9 13.2 subtract_bitcast_fusion.5
  282.1 7.8 fusion.10
  290.8 39.6 %all-reduce.7.cloned.1.call-done = f32[2,256,256]{2,1,0:T(8,128)} async-done(((f32[2,256,256]{2,1,0:T(8,128)}), f32[2,256,256]{2,1,0:T(8,128)}) %all-reduce.7.cloned.1.call-update) | async-done | bytes 524304 | tf_op jit(solution)/shard_map/psum | solution.py:45
  330.5 57.7 %all-reduce.9.cloned.1.call-done = f32[2,256,256]{2,1,0:T(8,128)} async-done(((f32[2,256,256]{2,1,0:T(8,128)}), f32[2,256,256]{2,1,0:T(8,128)}) %all-reduce.9.cloned.1.call-update) | async-done | bytes 524304 | tf_op jit(solution)/shard_map/psum | solution.py:45
  390.3 6.1 fusion.21
  436.8 6.9 fusion.3
  443.7 8.3 copy.81
  451.9 187.2 %all_to_all.99 = f32[16,2,256,256]{3,0,1,2:T(8,128)S(1)} all-to-all(f32[16,2,256,256]{3,0,1,2:T(8,128)} %copy.81), channel_id=1, replica_groups=mesh['mode'=8,'orb'=4] {'orb'}, dimensions={2} | all-to-all | bytes 16777216 | tf_op jit(solution)/shard_map/all_to_all | solution.py:55
  639.2 8.3 copy.145
  647.4 9.4 reshape.18
  656.8 11.6 copy.83
  674.1 56.8 %all-gather.2.cloned.1.call-done = f32[512,512]{1,0:T(8,128)} async-done(((f32[64,512]{1,0:T(8,128)}), f32[512,512]{1,0:T(8,128)}) %all-gather.2.cloned.1.call-update) | async-done | bytes 1048592 | tf_op jit(solution)/shard_map/all_gather | solution.py:64
  731.0 40.7 %all-to-all-done.2 = f32[64,8,4096]{2,0,1:T(8,128)} async-done(((f32[64,8,4096]{2,0,1:T(8,128)}), f32[64,8,4096]{2,0,1:T(8,128)}, u32[]{:S(2)}, u32[]{:S(2)}) %all-to-all-start.2) | async-done | bytes 8388640 | tf_op jit(solution)/shard_map/all_to_all | solution.py:62
  771.6 30.3 %convolution_bitcast_fusion = f32[512,1,4096]{0,2,1:T(8,128)} fusion(f32[512,4096]{1,0:T(8,128)} %bitcast.41, f32[512,512]{1,0:T(8,128)} %all-gather.2.cloned.1.call-done), kind=kOutput, calls=%fused_computation.19 | convolution fusion | flops 12884901888 | bytes 17825792 | tf_op jit(solution)/shard_map/mn,nx->mx/dot_general | solution.py:11
  801.9 19.3 %copy.84 = f32[512,1,4096]{2,1,0:T(1,128)} copy(f32[512,1,4096]{0,2,1:T(8,128)} %convolution_bitcast_fusion) | data formatting | bytes 16777216 | tf_op jit(solution)/shard_map/broadcast_in_dim | solution.py:65
  821.2 97.8 %all_to_all.100 = f32[512,1,4096]{2,1,0:T(1,128)S(1)} all-to-all(f32[512,1,4096]{2,1,0:T(1,128)} %copy.84), channel_id=1, replica_groups=mesh['mode'=8,'orb'=4] {'mode'}, dimensions={0} | all-to-all | bytes 16777216 | tf_op jit(solution)/shard_map/all_to_all | solution.py:65
  919.0 8.1 copy.134
  927.1 8.5 copy.85
  935.5 9.4 reshape.19
  944.9 5.7 all-to-all-start.4
  950.6 12.5 fusion.8
  964.5 75.9 %all-reduce.11.cloned.1.call-done = f32[2,256,256]{2,1,0:T(8,128)} async-done(((f32[2,256,256]{2,1,0:T(8,128)}), f32[2,256,256]{2,1,0:T(8,128)}) %all-reduce.11.cloned.1.call-update) | async-done | bytes 524304 | tf_op jit(solution)/shard_map/psum | solution.py:45
  1040.4 124.8 %all-reduce.13.cloned.1.call-done = f32[2,256,256]{2,1,0:T(8,128)} async-done(((f32[2,256,256]{2,1,0:T(8,128)}), f32[2,256,256]{2,1,0:T(8,128)}) %all-reduce.13.cloned.1.call-update) | async-done | bytes 524304 | tf_op jit(solution)/shard_map/psum | solution.py:45
  1214.4 8.3 copy.95
  1222.7 5.6 all-to-all-start.5
  1228.4 12.7 fusion.6
  1242.0 74.7 %all-reduce.15.cloned.1.call-done = f32[2,256,256]{2,1,0:T(8,128)} async-done(((f32[2,256,256]{2,1,0:T(8,128)}), f32[2,256,256]{2,1,0:T(8,128)}) %all-reduce.15.cloned.1.call-update) | async-done | bytes 524304 | tf_op jit(solution)/shard_map/psum | solution.py:45
  1316.6 125.9 %all-reduce.17.cloned.1.call-done = f32[2,256,256]{2,1,0:T(8,128)} async-done(((f32[2,256,256]{2,1,0:T(8,128)}), f32[2,256,256]{2,1,0:T(8,128)}) %all-reduce.17.cloned.1.call-update) | async-done | bytes 524304 | tf_op jit(solution)/shard_map/psum | solution.py:45
  1444.1 11.6 copy.96
  (93 shorter events, 147.3 us)
Async XLA Ops:
  7.2 6.5 copy-start.14
  7.2 6.6 copy-start.12
  7.2 200.5 %copy-start.13 = (f32[2,64,256]{2,1,0:T(8,128)S(1)}, f32[2,64,256]{2,1,0:T(8,128)}, u32[]{:S(2)}) copy-start(f32[2,64,256]{2,1,0:T(8,128)} %param.7) | copy-start | bytes 393220
  7.2 216.6 %all-to-all-start = ((f32[64,2,64,256]{3,2,1,0:T(8,128)}), f32[64,2,64,256]{3,2,1,0:T(8,128)}, u32[]{:S(2)}, u32[]{:S(2)}) async-start(f32[64,2,64,256]{3,2,1,0:T(8,128)} %param.5), calls=%async_computation | async-start | bytes 16777216 | tf_op jit(solution)/shard_map/all_to_all | solution.py:51
  13.7 316.8 %all-reduce.7.cloned.1.call-start = ((), (), s32[]{:S(2)}) async-start(), calls=%async_computation.6 | async-start | bytes 1048576 | tf_op jit(solution)/shard_map/psum | solution.py:45
  207.7 180.5 %copy-start.8 = (f32[2,256,256]{2,1,0:T(8,128)}, f32[2,256,256]{2,1,0:T(8,128)S(1)}, u32[]{:S(2)}) copy-start(f32[2,256,256]{2,1,0:T(8,128)S(1)} %all_gather.10) | copy-start | bytes 1572868
  223.7 164.5 %copy-start.9 = (f32[2,256,256]{2,1,0:T(8,128)}, f32[2,256,256]{2,1,0:T(8,128)S(1)}, u32[]{:S(2)}) copy-start(f32[2,256,256]{2,1,0:T(8,128)S(1)} %all_gather.9) | copy-start | bytes 1572868
  227.9 45.9 %copy-start = (f32[4,16,2,64,256]{4,3,0,1,2:T(8,128)}, f32[4,16,2,64,256]{4,3,0,1,2:T(8,128)S(1)}, u32[]{:S(2)}) copy-start(f32[4,16,2,64,256]{4,3,0,1,2:T(8,128)S(1)} %copy.64) | copy-start | bytes 25165828
  273.8 4.9 copy-start.5
  278.7 3.4 copy-start.1
  290.8 97.4 %all-reduce.9.cloned.1.call-start = ((), (), s32[]{:S(2)}) async-start(), calls=%async_computation.7 | async-start | bytes 1048576 | tf_op jit(solution)/shard_map/psum | solution.py:45
  388.2 8.2 copy-start.2
  422.7 5.4 copy-start.7
  422.7 14.0 slice-start
  428.2 8.6 slice-start.1
  432.5 4.3 copy-start.6
  443.6 8.3 copy-start.3
  668.4 103.2 %all-to-all-start.2 = ((f32[64,8,4096]{2,0,1:T(8,128)}), f32[64,8,4096]{2,0,1:T(8,128)}, u32[]{:S(2)}, u32[]{:S(2)}) async-start(f32[64,8,4096]{2,0,1:T(8,128)} %copy.83), calls=%async_computation.2 | async-start | bytes 16777216 | tf_op jit(solution)/shard_map/all_to_all | solution.py:62
  673.4 57.6 %all-gather.2.cloned.1.call-start = ((), (), s32[]{:S(2)}) async-start(), calls=%async_computation.8 | async-start | bytes 1179648 | tf_op jit(solution)/shard_map/all_gather | solution.py:64
  944.9 221.4 %all-to-all-start.4 = ((f32[64,2,64,256]{3,2,1,0:T(8,128)}), f32[64,2,64,256]{3,2,1,0:T(8,128)}, u32[]{:S(2)}, u32[]{:S(2)}) async-start(f32[64,2,64,256]{3,2,1,0:T(8,128)} %reshape.19), calls=%async_computation.4 | async-start | bytes 16777216 | tf_op jit(solution)/shard_map/all_to_all | solution.py:51
  950.6 214.6 %copy-start.10 = (f32[2,256,256]{2,1,0:T(8,128)S(1)}, f32[2,256,256]{2,1,0:T(8,128)}, u32[]{:S(2)}) copy-start(f32[2,256,256]{2,1,0:T(8,128)} %copy-done.9) | copy-start | bytes 1572868
  950.6 214.6 %copy-start.11 = (f32[2,256,256]{2,1,0:T(8,128)S(1)}, f32[2,256,256]{2,1,0:T(8,128)}, u32[]{:S(2)}) copy-start(f32[2,256,256]{2,1,0:T(8,128)} %get-tuple-element.5) | copy-start | bytes 1572868
  950.6 89.8 %all-reduce.11.cloned.1.call-start = ((), (), s32[]{:S(2)}) async-start(), calls=%async_computation.9 | async-start | bytes 1048576 | tf_op jit(solution)/shard_map/psum | solution.py:45
  964.0 201.1 %all-reduce.13.cloned.1.call-start = ((), (), s32[]{:S(2)}) async-start(), calls=%async_computation.10 | async-start | bytes 1048576 | tf_op jit(solution)/shard_map/psum | solution.py:45
  1211.2 3.3 copy-start.4
  1222.7 221.4 %all-to-all-start.5 = ((f32[16,2,256,256]{3,0,1,2:T(8,128)}), f32[16,2,256,256]{3,0,1,2:T(8,128)}, u32[]{:S(2)}, u32[]{:S(2)}) async-start(f32[16,2,256,256]{3,0,1,2:T(8,128)} %copy.95), calls=%async_computation.5 | async-start | bytes 16777216 | tf_op jit(solution)/shard_map/all_to_all | solution.py:55
  1228.3 88.3 %all-reduce.15.cloned.1.call-start = ((), (), s32[]{:S(2)}) async-start(), calls=%async_computation.11 | async-start | bytes 1048576 | tf_op jit(solution)/shard_map/psum | solution.py:45
  1241.9 200.6 %all-reduce.17.cloned.1.call-start = ((), (), s32[]{:S(2)}) async-start(), calls=%async_computation.12 | async-start | bytes 1048576 | tf_op jit(solution)/shard_map/psum | solution.py:45
Sparse Core Ops, SparseCore 0:
  290.9 39.5 all-reduce.6
  333.5 54.6 all-reduce.8
  676.1 54.8 all-gather.1
  964.1 76.1 all-reduce.10
  1043.3 121.7 all-reduce.12
  1242.0 74.5 all-reduce.14
  1319.7 122.7 all-reduce.16
